TPU v7x, 256 devices: a whole 4x4x8 slice. The times are simulated.
256 devices in a mesh: section: 8 (over z_lo, x), replica: 32 (over y, z_hi, core).
Axes of the slice: x: 4, y: 4, z: 8 (z_hi: 4, z_lo: 2; z = z_hi * 2 + z_lo), core: 2. Of those that a mesh axis runs over, the one named last changes fastest.
Arguments:
- inputs: bfloat16 [32, 2, 64, 2048], P('replica', None, 'section'), may hold values from -6 to 6
- cotangent: bfloat16 [32, 2, 64, 2048], P('replica', None, 'section'), may hold values from -6 to 6
- gate_weight: bfloat16 [8, 32, 2048, 768], P('section', 'replica'), may hold values from -0.125 to 0.125
- up_weight: bfloat16 [8, 32, 2048, 768], P('section', 'replica'), may hold values from -0.125 to 0.125
- down_weight: bfloat16 [8, 32, 768, 2048], P('section', 'replica'), may hold values from -0.21875 to 0.21875
- momentum: float32 [8, 32, 128, 768], P('section', 'replica'), may hold values from -6 to 6
- routes: int32 [7, 2, 32], replicated, may hold values from 0 to 31, each once within a row
- pairing: int32 [8, 32], replicated, may hold values from 0 to 31, as said below
Outputs:
- activations: bfloat16 [8, 32, 2, 64, 2048], P('section', 'replica')
- input_grads: bfloat16 [8, 32, 2, 64, 2048], P('section', 'replica')
- buckets: float32 [8, 32, 128, 768], P('section', 'replica')
Inputs may be any that keep to these rules, and one draw needn't show every extreme that they name: routes[s, m] is a permutation of the 32 replicas. pairing[s] splits the 32 replicas into pairs: pairing[s, pairing[s, r]] = r and pairing[s, r] != r.
All inputs are finite; a program needn't handle non-finite values.
Results may differ from a plain program's by a relative error of at most 0.028.
Values may be sent and summed in bfloat16 or wider, within the bound.
A program may use at most 64 MiB of HBM per device.

v0:
```python
import jax
import jax.numpy as jnp
from jax import lax
from jax.sharding import PartitionSpec as P

EPS = 1e-06
BETA = 0.9


def passed_along(block, axis, distance):
    devices = range(lax.axis_size(axis))
    route = [(i - distance, i) for i in devices if i - distance in devices]
    return lax.ppermute(block, axis, route)


def normalize(af):
    rinv = lax.rsqrt(jnp.mean(af * af, axis=-1, keepdims=True) + EPS)
    return (af * rinv, rinv)


def expert_forward(block, gate, up, down):
    af = block.astype(jnp.float32)
    normed, rinv = normalize(af)
    narrow = normed.astype(jnp.bfloat16)
    gated = jnp.dot(narrow, gate, preferred_element_type=jnp.float32)
    upward = jnp.dot(narrow, up, preferred_element_type=jnp.float32)
    hidden = (jax.nn.silu(gated) * upward).astype(jnp.bfloat16)
    return (af + jnp.dot(hidden, down, preferred_element_type=jnp.float32)).astype(jnp.bfloat16)


def contract_last(left, right):
    return lax.dot_general(
        left, right, (((1,), (1,)), ((), ())), preferred_element_type=jnp.float32
    )


def expert_backward(block, dout, gate, up, down, bucket_rows):
    af = block.astype(jnp.float32)
    normed, rinv = normalize(af)
    narrow = normed.astype(jnp.bfloat16)
    gated = jnp.dot(narrow, gate, preferred_element_type=jnp.float32)
    upward = jnp.dot(narrow, up, preferred_element_type=jnp.float32)
    sigma = jax.nn.sigmoid(gated)
    dhidden = contract_last(dout, down)
    dgate = (dhidden * upward * sigma * (1.0 + gated * (1.0 - sigma))).astype(jnp.bfloat16)
    dup = (dhidden * gated * sigma).astype(jnp.bfloat16)
    dnorm = contract_last(dgate, gate) + contract_last(dup, up)
    dinput = dout.astype(jnp.float32) + rinv * (
        dnorm - normed * jnp.mean(dnorm * normed, axis=-1, keepdims=True)
    )
    part = lax.dot_general(
        narrow[:, :bucket_rows], dgate, (((0,), (0,)), ((), ())), preferred_element_type=jnp.float32
    )
    return (dinput.astype(jnp.bfloat16), part)


def inverse_of(perm):
    count = perm.shape[0]
    series = jnp.arange(count, dtype=jnp.int32)
    hits = perm[:, None] == series[None, :]
    return jnp.sum(jnp.where(hits, series[:, None], 0), axis=0)


def route(block, anchor):
    count = lax.axis_size("replica")
    pieces = block.reshape((count, block.shape[0] // count) + block.shape[1:])
    spread = lax.all_to_all(pieces, "replica", split_axis=0, concat_axis=0, tiled=True)
    ordered = jnp.take(spread, anchor, axis=0)
    back = lax.all_to_all(ordered, "replica", split_axis=0, concat_axis=0, tiled=True)
    return back.reshape(block.shape)


def step_section(block, offset):
    return passed_along(block, "section", offset)


def local(inputs, cotangent, gate_weight, up_weight, down_weight, momentum, routes, pairing):
    gate = gate_weight[0, 0]
    up = up_weight[0, 0]
    down = down_weight[0, 0]
    own_momentum = momentum[0, 0]
    bucket_rows = own_momentum.shape[0]
    sections = lax.axis_size("section")
    section = lax.axis_index("section")
    whole_in, whole_cot = (
        lax.all_gather(inputs[0], "section", axis=1, tiled=True),
        lax.all_gather(cotangent[0], "section", axis=1, tiled=True),
    )
    micro, rows, width = whole_in.shape
    parts = 1
    units = micro * parts
    unit_rows = rows // parts
    route_section = jnp.clip(section, 0, routes.shape[0] - 1)
    steps = sections + units - 1
    empty = jnp.zeros((units, unit_rows, width), jnp.bfloat16)
    blank = jnp.zeros((unit_rows, width), jnp.bfloat16)

    def forward_step(step, carry):
        incoming, saved_in, saved_out = carry
        unit = step - section
        valid = (unit >= 0) & (unit < units)
        slot = jnp.clip(unit, 0, units - 1)
        fresh = lax.dynamic_index_in_dim(whole_in, slot, 0, keepdims=False)
        block = jnp.where(section == 0, fresh, incoming)
        result = lax.cond(
            valid, lambda: expert_forward(block, gate, up, down), lambda: jnp.zeros_like(block)
        )
        kept_in = lax.dynamic_index_in_dim(saved_in, slot, 0, keepdims=False)
        kept_out = lax.dynamic_index_in_dim(saved_out, slot, 0, keepdims=False)
        saved_in = lax.dynamic_update_index_in_dim(
            saved_in, jnp.where(valid, block, kept_in), slot, 0
        )
        saved_out = lax.dynamic_update_index_in_dim(
            saved_out, jnp.where(valid, result, kept_out), slot, 0
        )
        anchor = inverse_of(routes[route_section, slot // parts])
        moved = route(result, anchor)
        return (step_section(moved, 1), saved_in, saved_out)

    _, saved_in, saved_out = lax.fori_loop(0, steps, forward_step, (blank, empty, empty))
    zero_part = jnp.zeros(own_momentum.shape, jnp.float32)

    def backward_step(step, carry):
        incoming, saved_grad, total = carry
        unit = step - (sections - 1 - section)
        valid = (unit >= 0) & (unit < units)
        slot = jnp.clip(unit, 0, units - 1)
        fresh = lax.dynamic_index_in_dim(whole_cot, slot, 0, keepdims=False)
        dout = jnp.where(section == sections - 1, fresh, incoming)
        block = lax.dynamic_index_in_dim(saved_in, slot, 0, keepdims=False)
        grad, part = lax.cond(
            valid,
            lambda: expert_backward(block, dout, gate, up, down, bucket_rows),
            lambda: (jnp.zeros_like(dout), zero_part),
        )
        kept = lax.dynamic_index_in_dim(saved_grad, slot, 0, keepdims=False)
        saved_grad = lax.dynamic_update_index_in_dim(
            saved_grad, jnp.where(valid, grad, kept), slot, 0
        )
        total = total + part
        sent = step_section(grad, -1)
        sender = jnp.clip(step - (sections - 2 - section), 0, units - 1)
        anchor = routes[route_section, sender // parts]
        return (route(sent, anchor), saved_grad, total)

    _, saved_grad, total = lax.fori_loop(0, steps, backward_step, (blank, empty, zero_part))
    fresh_bucket = (BETA * own_momentum + (1.0 - BETA) * total).astype(jnp.bfloat16)
    partner = route(fresh_bucket, pairing[section])
    buckets = 0.5 * (fresh_bucket.astype(jnp.float32) + partner.astype(jnp.float32))
    activations = saved_out.reshape(1, 1, micro, rows, width)
    input_grads = saved_grad.reshape(1, 1, micro, rows, width)
    return (activations, input_grads, buckets[None, None])


def solution(mesh):
    placed = (
        P("replica", None, "section", None),
        P("replica", None, "section", None),
        P("section", "replica", None, None),
        P("section", "replica", None, None),
        P("section", "replica", None, None),
        P("section", "replica", None, None),
        P(),
        P(),
    )
    return jax.shard_map(
        local,
        mesh=mesh,
        in_specs=placed,
        out_specs=(
            P("section", "replica", None, None, None),
            P("section", "replica", None, None, None),
            P("section", "replica", None, None),
        ),
        check_vma=False,
    )
```

profile of v0, /device:TPU:25, one launch (start us, length us, event | category | flops | bytes accessed | tf_op | source)
XLA Modules:
  0.0 1151.8 jit_solution(4088261014999258927)
XLA Ops:
  0.7 26.0 %all-gather = bf16[1,2,64,2048]{3,2,1,0:T(8,128)(2,1)} all-gather(bf16[1,2,8,2048]{3,2,1,0:T(8,128)(2,1)} %param.18), channel_id=2, replica_groups=mesh['section'=8,'replica'=32] {'section'}, dimensions={2}, use_global_device_ids=true | all-gather | bytes 589824 | tf_op jit(solution)/shard_map/all_gather | solution.py:86
  26.7 25.6 %all-gather.1 = bf16[1,2,64,2048]{3,2,1,0:T(8,128)(2,1)} all-gather(bf16[1,2,8,2048]{3,2,1,0:T(8,128)(2,1)} %param.19), channel_id=3, replica_groups=mesh['section'=8,'replica'=32] {'section'}, dimensions={2}, use_global_device_ids=true | all-gather | bytes 589824 | tf_op jit(solution)/shard_map/all_gather | solution.py:87
  54.7 515.6 %while.43 = (s32[]{:T(128)}, bf16[64,2048]{1,0:T(8,128)(2,1)}, bf16[2,64,2048]{2,1,0:T(8,128)(2,1)}, bf16[2,64,2048]{2,1,0:T(8,128)(2,1)}, s32[]{:T(128)}, /*ind...) while((s32[]{:T(128)}, bf16[64,2048]{1,0:T(8,128)(2,1)}, ...), condition=%wide.region_5.7_spmd, body=%wide.region_0.6_spmd.sunk | while | flops 606376256 | bytes 35528072 | solution.py:120
  67.2 22.5 %all-to-all-start = ((bf16[32,2,2048]{2,1,0:T(2,128)(2,1)}), bf16[32,2,2048]{2,1,0:T(2,128)(2,1)S(1)}, u32[]{:S(2)}, u32[]{:S(2)}) async-start(bf16[32,2,2048]{2,1,0:T(2,128)(2,1)} %reshape.181), calls=%async_computation | async-start | bytes 524288 | tf_op jit(solution)/shard_map/while/body/eval_jaxpr/all_to_all | solution.py:67
  225.1 13.1 %collective-permute-start = (bf16[64,2048]{1,0:T(8,128)(2,1)S(1)}, bf16[64,2048]{1,0:T(8,128)(2,1)}, u32[]{:S(2)}, u32[]{:S(2)}) collective-permute-start(bf16[64,2048]{1,0:T(8,128)(2,1)S(1)} %reshape.182), channel_id=1, source_target_pairs={{0,32},{32,64},{64,96},{96,128},{128,160},{160,192},{192,224},{1,3... | collective-permute-start | bytes 786440 | tf_op jit(solution)/shard_map/while/body/eval_jaxpr/ppermute | solution.py:13
  382.0 10.7 all-to-all-done.1
  489.5 10.7 all-to-all-done.1
  542.4 10.7 all-to-all-done.1
  553.2 12.2 %collective-permute-start = (bf16[64,2048]{1,0:T(8,128)(2,1)S(1)}, bf16[64,2048]{1,0:T(8,128)(2,1)}, u32[]{:S(2)}, u32[]{:S(2)}) collective-permute-start(bf16[64,2048]{1,0:T(8,128)(2,1)S(1)} %reshape.182), channel_id=1, source_target_pairs={{0,32},{32,64},{64,96},{96,128},{128,160},{160,192},{192,224},{1,3... | collective-permute-start | bytes 786440 | tf_op jit(solution)/shard_map/while/body/eval_jaxpr/ppermute | solution.py:13
  570.4 547.2 %while.44 = (s32[]{:T(128)}, bf16[64,2048]{1,0:T(8,128)(2,1)S(1)}, bf16[2,64,2048]{2,1,0:T(8,128)(2,1)S(1)}, f32[128,768]{1,0:T(8,128)}, s32[]{:T(128)}, /*index...) while((s32[]{:T(128)}, bf16[64,2048]{1,0:T(8,128)(2,1)S(1)}, ...), condition=%wide.region_11.13_spmd.clone, body=%wide.region_6.12_spmd.clone.sunk | while | flops 1023214848 | bytes 73064136 | solution.py:146
  571.9 10.7 collective-permute-done.1
  621.3 12.0 %collective-permute-done.1 = bf16[64,2048]{1,0:T(8,128)(2,1)S(1)} collective-permute-done((bf16[64,2048]{1,0:T(8,128)(2,1)S(1)}, bf16[64,2048]{1,0:T(8,128)(2,1)S(1)}, u32[]{:S(2)}, u32[]{:S(2)}) %collective-permute-start.1) | collective-permute-done | bytes 262176 | tf_op jit(solution)/shard_map/while/body/eval_jaxpr/ppermute | solution.py:13
  671.2 13.2 %collective-permute-done.1 = bf16[64,2048]{1,0:T(8,128)(2,1)S(1)} collective-permute-done((bf16[64,2048]{1,0:T(8,128)(2,1)S(1)}, bf16[64,2048]{1,0:T(8,128)(2,1)S(1)}, u32[]{:S(2)}, u32[]{:S(2)}) %collective-permute-start.1) | collective-permute-done | bytes 262176 | tf_op jit(solution)/shard_map/while/body/eval_jaxpr/ppermute | solution.py:13
  722.3 13.5 %collective-permute-done.1 = bf16[64,2048]{1,0:T(8,128)(2,1)S(1)} collective-permute-done((bf16[64,2048]{1,0:T(8,128)(2,1)S(1)}, bf16[64,2048]{1,0:T(8,128)(2,1)S(1)}, u32[]{:S(2)}, u32[]{:S(2)}) %collective-permute-start.1) | collective-permute-done | bytes 262176 | tf_op jit(solution)/shard_map/while/body/eval_jaxpr/ppermute | solution.py:13
  773.7 11.5 collective-permute-done.1
  793.0 10.8 all-to-all-done.2
  811.9 11.6 %all-to-all-done.3 = bf16[32,2,2048]{2,1,0:T(2,128)(2,1)S(1)} async-done(((bf16[32,2,2048]{2,1,0:T(2,128)(2,1)}), bf16[32,2,2048]{2,1,0:T(2,128)(2,1)S(1)}, u32[]{:S(2)}, u32[]{:S(2)}) %all-to-all-start.3) | async-done | bytes 262176 | tf_op jit(solution)/shard_map/while/body/eval_jaxpr/all_to_all | solution.py:69
  873.9 85.1 %collective-permute-done.1 = bf16[64,2048]{1,0:T(8,128)(2,1)S(1)} collective-permute-done((bf16[64,2048]{1,0:T(8,128)(2,1)S(1)}, bf16[64,2048]{1,0:T(8,128)(2,1)S(1)}, u32[]{:S(2)}, u32[]{:S(2)}) %collective-permute-start.1) | collective-permute-done | bytes 262176 | tf_op jit(solution)/shard_map/while/body/eval_jaxpr/ppermute | solution.py:13
  985.0 10.7 all-to-all-done.3
  995.9 11.6 %conditional.6 = (bf16[64,2048]{1,0:T(8,128)(2,1)S(1)}, f32[128,768]{1,0:T(8,128)S(1)}) conditional(s32[]{:T(128)} %convert_element_type.119, () %tuple.125, (pred[]{:T(512)}, bf16[2,64,2048]{2,1,0:T(8,128)(2,1)}, s32[]{:T(128)}, bf16[64,2048]{1,0:T(8,128)(2,1)S(1)}, bf16[2,64,2048]{2,1,0:T(8,128)(2,1)}, /*index=5*/bf16[768,2048]{1,0:T(8,128)(2,1)}, ...), branch_computations={%region_7.8_spmd, %region_8.11_spmd} | conditional | flops 1022754880 | bytes 62704276 | solution.py:131
  1008.9 13.8 %collective-permute-done.1 = bf16[64,2048]{1,0:T(8,128)(2,1)S(1)} collective-permute-done((bf16[64,2048]{1,0:T(8,128)(2,1)S(1)}, bf16[64,2048]{1,0:T(8,128)(2,1)S(1)}, u32[]{:S(2)}, u32[]{:S(2)}) %collective-permute-start.1) | collective-permute-done | bytes 262176 | tf_op jit(solution)/shard_map/while/body/eval_jaxpr/ppermute | solution.py:13
  1059.1 11.6 %conditional.6 = (bf16[64,2048]{1,0:T(8,128)(2,1)S(1)}, f32[128,768]{1,0:T(8,128)S(1)}) conditional(s32[]{:T(128)} %convert_element_type.119, () %tuple.125, (pred[]{:T(512)}, bf16[2,64,2048]{2,1,0:T(8,128)(2,1)}, s32[]{:T(128)}, bf16[64,2048]{1,0:T(8,128)(2,1)S(1)}, bf16[2,64,2048]{2,1,0:T(8,128)(2,1)}, /*index=5*/bf16[768,2048]{1,0:T(8,128)(2,1)}, ...), branch_computations={%region_7.8_spmd, %region_8.11_spmd} | conditional | flops 1022754880 | bytes 62704276 | solution.py:131
  1106.7 10.8 all-to-all-done.3
  1136.0 14.9 %all_to_all.72 = bf16[32,4,768]{2,1,0:T(4,128)(2,1)S(1)} all-to-all(bf16[32,4,768]{2,1,0:T(4,128)(2,1)S(1)} %broadcast_select_fusion.2), channel_id=1, replica_groups=mesh['section'=8,'replica'=32] {'replica'}, dimensions={0} | all-to-all | bytes 393216 | tf_op jit(solution)/shard_map/all_to_all | solution.py:69
  (469 shorter events, 819.7 us)
Async XLA Ops:
  67.2 33.2 %all-to-all-start = ((bf16[32,2,2048]{2,1,0:T(2,128)(2,1)}), bf16[32,2,2048]{2,1,0:T(2,128)(2,1)S(1)}, u32[]{:S(2)}, u32[]{:S(2)}) async-start(bf16[32,2,2048]{2,1,0:T(2,128)(2,1)} %reshape.181), calls=%async_computation | async-start | bytes 524288 | tf_op jit(solution)/shard_map/while/body/eval_jaxpr/all_to_all | solution.py:67
  138.6 16.8 %all-to-all-start = ((bf16[32,2,2048]{2,1,0:T(2,128)(2,1)}), bf16[32,2,2048]{2,1,0:T(2,128)(2,1)S(1)}, u32[]{:S(2)}, u32[]{:S(2)}) async-start(bf16[32,2,2048]{2,1,0:T(2,128)(2,1)} %reshape.181), calls=%async_computation | async-start | bytes 524288 | tf_op jit(solution)/shard_map/while/body/eval_jaxpr/all_to_all | solution.py:67
  189.4 16.9 %all-to-all-start = ((bf16[32,2,2048]{2,1,0:T(2,128)(2,1)}), bf16[32,2,2048]{2,1,0:T(2,128)(2,1)S(1)}, u32[]{:S(2)}, u32[]{:S(2)}) async-start(bf16[32,2,2048]{2,1,0:T(2,128)(2,1)} %reshape.181), calls=%async_computation | async-start | bytes 524288 | tf_op jit(solution)/shard_map/while/body/eval_jaxpr/all_to_all | solution.py:67
  225.1 18.1 %collective-permute-start = (bf16[64,2048]{1,0:T(8,128)(2,1)S(1)}, bf16[64,2048]{1,0:T(8,128)(2,1)}, u32[]{:S(2)}, u32[]{:S(2)}) collective-permute-start(bf16[64,2048]{1,0:T(8,128)(2,1)S(1)} %reshape.182), channel_id=1, source_target_pairs={{0,32},{32,64},{64,96},{96,128},{128,160},{160,192},{192,224},{1,3... | collective-permute-start | bytes 786440 | tf_op jit(solution)/shard_map/while/body/eval_jaxpr/ppermute | solution.py:13
  248.5 16.9 %all-to-all-start = ((bf16[32,2,2048]{2,1,0:T(2,128)(2,1)}), bf16[32,2,2048]{2,1,0:T(2,128)(2,1)S(1)}, u32[]{:S(2)}, u32[]{:S(2)}) async-start(bf16[32,2,2048]{2,1,0:T(2,128)(2,1)} %reshape.181), calls=%async_computation | async-start | bytes 524288 | tf_op jit(solution)/shard_map/while/body/eval_jaxpr/all_to_all | solution.py:67
  300.5 16.9 %all-to-all-start = ((bf16[32,2,2048]{2,1,0:T(2,128)(2,1)}), bf16[32,2,2048]{2,1,0:T(2,128)(2,1)S(1)}, u32[]{:S(2)}, u32[]{:S(2)}) async-start(bf16[32,2,2048]{2,1,0:T(2,128)(2,1)} %reshape.181), calls=%async_computation | async-start | bytes 524288 | tf_op jit(solution)/shard_map/while/body/eval_jaxpr/all_to_all | solution.py:67
  356.1 16.9 %all-to-all-start = ((bf16[32,2,2048]{2,1,0:T(2,128)(2,1)}), bf16[32,2,2048]{2,1,0:T(2,128)(2,1)S(1)}, u32[]{:S(2)}, u32[]{:S(2)}) async-start(bf16[32,2,2048]{2,1,0:T(2,128)(2,1)} %reshape.181), calls=%async_computation | async-start | bytes 524288 | tf_op jit(solution)/shard_map/while/body/eval_jaxpr/all_to_all | solution.py:67
  375.1 17.5 %all-to-all-start.1 = ((bf16[32,2,2048]{2,1,0:T(2,128)(2,1)}), bf16[32,2,2048]{2,1,0:T(2,128)(2,1)S(1)}, u32[]{:S(2)}, u32[]{:S(2)}) async-start(bf16[32,2,2048]{2,1,0:T(2,128)(2,1)} %broadcast_select_fusion.5), calls=%async_computation.1 | async-start | bytes 524288 | tf_op jit(solution)/shard_map/while/body/eval_jaxpr/all_to_all | solution.py:69
  406.9 17.1 %all-to-all-start = ((bf16[32,2,2048]{2,1,0:T(2,128)(2,1)}), bf16[32,2,2048]{2,1,0:T(2,128)(2,1)S(1)}, u32[]{:S(2)}, u32[]{:S(2)}) async-start(bf16[32,2,2048]{2,1,0:T(2,128)(2,1)} %reshape.181), calls=%async_computation | async-start | bytes 524288 | tf_op jit(solution)/shard_map/while/body/eval_jaxpr/all_to_all | solution.py:67
  426.2 17.4 %all-to-all-start.1 = ((bf16[32,2,2048]{2,1,0:T(2,128)(2,1)}), bf16[32,2,2048]{2,1,0:T(2,128)(2,1)S(1)}, u32[]{:S(2)}, u32[]{:S(2)}) async-start(bf16[32,2,2048]{2,1,0:T(2,128)(2,1)} %broadcast_select_fusion.5), calls=%async_computation.1 | async-start | bytes 524288 | tf_op jit(solution)/shard_map/while/body/eval_jaxpr/all_to_all | solution.py:69
  463.6 16.9 %all-to-all-start = ((bf16[32,2,2048]{2,1,0:T(2,128)(2,1)}), bf16[32,2,2048]{2,1,0:T(2,128)(2,1)S(1)}, u32[]{:S(2)}, u32[]{:S(2)}) async-start(bf16[32,2,2048]{2,1,0:T(2,128)(2,1)} %reshape.181), calls=%async_computation | async-start | bytes 524288 | tf_op jit(solution)/shard_map/while/body/eval_jaxpr/all_to_all | solution.py:67
  482.7 17.5 %all-to-all-start.1 = ((bf16[32,2,2048]{2,1,0:T(2,128)(2,1)}), bf16[32,2,2048]{2,1,0:T(2,128)(2,1)S(1)}, u32[]{:S(2)}, u32[]{:S(2)}) async-start(bf16[32,2,2048]{2,1,0:T(2,128)(2,1)} %broadcast_select_fusion.5), calls=%async_computation.1 | async-start | bytes 524288 | tf_op jit(solution)/shard_map/while/body/eval_jaxpr/all_to_all | solution.py:69
  516.5 16.9 %all-to-all-start = ((bf16[32,2,2048]{2,1,0:T(2,128)(2,1)}), bf16[32,2,2048]{2,1,0:T(2,128)(2,1)S(1)}, u32[]{:S(2)}, u32[]{:S(2)}) async-start(bf16[32,2,2048]{2,1,0:T(2,128)(2,1)} %reshape.181), calls=%async_computation | async-start | bytes 524288 | tf_op jit(solution)/shard_map/while/body/eval_jaxpr/all_to_all | solution.py:67
  535.6 17.5 %all-to-all-start.1 = ((bf16[32,2,2048]{2,1,0:T(2,128)(2,1)}), bf16[32,2,2048]{2,1,0:T(2,128)(2,1)S(1)}, u32[]{:S(2)}, u32[]{:S(2)}) async-start(bf16[32,2,2048]{2,1,0:T(2,128)(2,1)} %broadcast_select_fusion.5), calls=%async_computation.1 | async-start | bytes 524288 | tf_op jit(solution)/shard_map/while/body/eval_jaxpr/all_to_all | solution.py:69
  553.2 17.1 %collective-permute-start = (bf16[64,2048]{1,0:T(8,128)(2,1)S(1)}, bf16[64,2048]{1,0:T(8,128)(2,1)}, u32[]{:S(2)}, u32[]{:S(2)}) collective-permute-start(bf16[64,2048]{1,0:T(8,128)(2,1)S(1)} %reshape.182), channel_id=1, source_target_pairs={{0,32},{32,64},{64,96},{96,128},{128,160},{160,192},{192,224},{1,3... | collective-permute-start | bytes 786440 | tf_op jit(solution)/shard_map/while/body/eval_jaxpr/ppermute | solution.py:13
  583.6 17.5 %all-to-all-start.2 = ((bf16[32,2,2048]{2,1,0:T(2,128)(2,1)}), bf16[32,2,2048]{2,1,0:T(2,128)(2,1)S(1)}, u32[]{:S(2)}, u32[]{:S(2)}) async-start(bf16[32,2,2048]{2,1,0:T(2,128)(2,1)} %reshape.185), calls=%async_computation.2 | async-start | bytes 524288 | tf_op jit(solution)/shard_map/while/body/eval_jaxpr/all_to_all | solution.py:67
  786.0 17.7 %all-to-all-start.2 = ((bf16[32,2,2048]{2,1,0:T(2,128)(2,1)}), bf16[32,2,2048]{2,1,0:T(2,128)(2,1)S(1)}, u32[]{:S(2)}, u32[]{:S(2)}) async-start(bf16[32,2,2048]{2,1,0:T(2,128)(2,1)} %reshape.185), calls=%async_computation.2 | async-start | bytes 524288 | tf_op jit(solution)/shard_map/while/body/eval_jaxpr/all_to_all | solution.py:67
  805.9 17.6 %all-to-all-start.3 = ((bf16[32,2,2048]{2,1,0:T(2,128)(2,1)}), bf16[32,2,2048]{2,1,0:T(2,128)(2,1)S(1)}, u32[]{:S(2)}, u32[]{:S(2)}) async-start(bf16[32,2,2048]{2,1,0:T(2,128)(2,1)} %broadcast_select_fusion.6), calls=%async_computation.3 | async-start | bytes 524288 | tf_op jit(solution)/shard_map/while/body/eval_jaxpr/all_to_all | solution.py:69
  836.7 17.0 %all-to-all-start.2 = ((bf16[32,2,2048]{2,1,0:T(2,128)(2,1)}), bf16[32,2,2048]{2,1,0:T(2,128)(2,1)S(1)}, u32[]{:S(2)}, u32[]{:S(2)}) async-start(bf16[32,2,2048]{2,1,0:T(2,128)(2,1)} %reshape.185), calls=%async_computation.2 | async-start | bytes 524288 | tf_op jit(solution)/shard_map/while/body/eval_jaxpr/all_to_all | solution.py:67
  872.5 86.5 %collective-permute-start.1 = (bf16[64,2048]{1,0:T(8,128)(2,1)S(1)}, bf16[64,2048]{1,0:T(8,128)(2,1)S(1)}, u32[]{:S(2)}, u32[]{:S(2)}) collective-permute-start(bf16[64,2048]{1,0:T(8,128)(2,1)S(1)} %get-tuple-element.1113), channel_id=1, source_target_pairs={{32,0},{64,32},{96,64},{128,96},{160,128},{192,160},{224,192},{33,... | collective-permute-start | bytes 786440 | tf_op jit(solution)/shard_map/while/body/eval_jaxpr/ppermute | solution.py:13
  959.9 16.9 %all-to-all-start.2 = ((bf16[32,2,2048]{2,1,0:T(2,128)(2,1)}), bf16[32,2,2048]{2,1,0:T(2,128)(2,1)S(1)}, u32[]{:S(2)}, u32[]{:S(2)}) async-start(bf16[32,2,2048]{2,1,0:T(2,128)(2,1)} %reshape.185), calls=%async_computation.2 | async-start | bytes 524288 | tf_op jit(solution)/shard_map/while/body/eval_jaxpr/all_to_all | solution.py:67
  978.9 16.9 %all-to-all-start.3 = ((bf16[32,2,2048]{2,1,0:T(2,128)(2,1)}), bf16[32,2,2048]{2,1,0:T(2,128)(2,1)S(1)}, u32[]{:S(2)}, u32[]{:S(2)}) async-start(bf16[32,2,2048]{2,1,0:T(2,128)(2,1)} %broadcast_select_fusion.6), calls=%async_computation.3 | async-start | bytes 524288 | tf_op jit(solution)/shard_map/while/body/eval_jaxpr/all_to_all | solution.py:69
  1081.4 17.2 %all-to-all-start.2 = ((bf16[32,2,2048]{2,1,0:T(2,128)(2,1)}), bf16[32,2,2048]{2,1,0:T(2,128)(2,1)S(1)}, u32[]{:S(2)}, u32[]{:S(2)}) async-start(bf16[32,2,2048]{2,1,0:T(2,128)(2,1)} %reshape.185), calls=%async_computation.2 | async-start | bytes 524288 | tf_op jit(solution)/shard_map/while/body/eval_jaxpr/all_to_all | solution.py:67
  1100.6 16.9 %all-to-all-start.3 = ((bf16[32,2,2048]{2,1,0:T(2,128)(2,1)}), bf16[32,2,2048]{2,1,0:T(2,128)(2,1)S(1)}, u32[]{:S(2)}, u32[]{:S(2)}) async-start(bf16[32,2,2048]{2,1,0:T(2,128)(2,1)} %broadcast_select_fusion.6), calls=%async_computation.3 | async-start | bytes 524288 | tf_op jit(solution)/shard_map/while/body/eval_jaxpr/all_to_all | solution.py:69
  (79 other events, 2079.6 us)
where the time goes:
time: 1160 us; the launch traced here: 1150 us
  waiting for transfers between devices  594 us (51%)
  starting transfers between devices  320 us (28%)
  local copies, waits for them, and re-layouts  80.2 us (7%)
  blocking collectives  66.6 us (6%)
  other arithmetic  56.8 us (5%)
  matrix products  30.9 us (3%)
    ppermute x18, waiting for transfers between devices, passed_along(): return lax.ppermute(block, axis, route)  221 us
    all_to_all x18, waiting for transfers between devices, route(): lax.all_to_all(ordered, 'replica', split_axis=0, concat_axis=0, tiled=True)  187 us
    all_to_all x19, waiting for transfers between devices, route(): lax.all_to_all(pieces, 'replica', split_axis=0, concat_axis=0, tiled=True)  186 us
    all_to_all x19, starting transfers between devices, route(): lax.all_to_all(pieces, 'replica', split_axis=0, concat_axis=0, tiled=True)  134 us
    all_to_all x18, starting transfers between devices, route(): lax.all_to_all(ordered, 'replica', split_axis=0, concat_axis=0, tiled=True)  105 us
    ppermute x18, starting transfers between devices, passed_along(): return lax.ppermute(block, axis, route)  80.3 us
    all_gather x1, blocking collectives, local(): lax.all_gather(inputs[0], 'section', axis=1, tiled=True)  26 us
    reshape x19, local copies, waits for them, and re-layouts, route(): pieces = block.reshape((count, block.shape[0] // count) + block.shape[1:])  25.9 us
  transfers between devices with their start and end apart: 55, of which 55 were waited for; matrix products, arithmetic and copies ran while one was open for 2% of the time, Pallas kernels for 0%

commit v1 on v0

v1 whole, which is shorter than its diff:
```python
import jax
import jax.numpy as jnp
from jax import lax
from jax.experimental import pallas as pl
from jax.experimental.pallas import tpu as pltpu
from jax.sharding import PartitionSpec as P

EPS = 1e-06
BETA = 0.9
MESH = pl.DeviceIdType.MESH
F32, BF16 = jnp.float32, jnp.bfloat16
SECTIONS, REPLICAS, MICRO, ROWS, D, FF, BUCKET = 8, 32, 2, 64, 2048, 768, 128
PR, PC = 32, 128
CHUNK = 256
BP = (BUCKET // PR) * (FF // PC)


def contract_last(a, b):
    return lax.dot_general(a, b, (((1,), (1,)), ((), ())), preferred_element_type=F32)


def kernel(inp, cot, gate_h, up_h, down_h, mom_h, routes_v, routes_s, pairing_s,
           act_h, ig_h, buck_h,
           gate, up, down, mom, gx, xd, out, p1a, p1b, p1c, p1d, p1e, snd, nbuf, rinv_b, g_b, u_b, a_b, b_b, total,
           fresh, partner, bucket, inv_v, inv_s,
           w_sem, m_sem, g_sem, gs_sem, p1_recv, p1_send, p2_recv, p2_send, o_sem, i_sem):
    t = lax.axis_index("section")
    r = lax.axis_index("replica")
    p1 = (p1a, p1b, p1c, p1d, p1e)
    relay_at = lax.rem(t + 4, SECTIONS)
    source = lax.rem(t + 4, SECTIONS)

    def dev(s, q):
        return {"section": s, "replica": q}

    def wait(ref, sem):
        pltpu.make_async_copy(ref, ref, sem).wait()

    loads = [pltpu.make_async_copy(h, v, w_sem.at[i])
             for i, (h, v) in enumerate(((gate_h.at[0, 0], gate), (up_h.at[0, 0], up), (down_h.at[0, 0], down)))]

    def gather(src, goal, sems):
        @pl.when(t == goal)
        def _():
            for m in range(MICRO):
                pltpu.make_async_copy(src.at[0, m], gx.at[m, t], g_sem.at[m]).start()

        @pl.when(t != goal)
        def _():
            for m in range(MICRO):
                pltpu.make_async_remote_copy(
                    src.at[0, m], gx.at[m, t], gs_sem.at[sems + m], g_sem.at[m],
                    device_id=dev(goal, r), device_id_type=MESH).start()

    gather(inp, 0, 0)
    for load in loads:
        load.start()
    gather(cot, SECTIONS - 1, MICRO)
    pltpu.make_async_copy(mom_h.at[0, 0], mom, m_sem).start()

    rv = routes_v[jnp.minimum(source, SECTIONS - 2)]
    goal_id = lax.broadcasted_iota(jnp.int32, (REPLICAS, REPLICAS), 0)
    from_id = lax.broadcasted_iota(jnp.int32, (REPLICAS, REPLICAS), 1)
    for m in range(MICRO):
        hit = rv[m:m + 1, :] == goal_id
        back = jnp.max(jnp.where(hit, from_id, 0), axis=1, keepdims=True)
        inv_v[m] = jnp.broadcast_to(back, (REPLICAS, 128))
    copy = pltpu.make_async_copy(inv_v, inv_s, i_sem)
    copy.start()
    copy.wait()

    def assemble(m, slot):
        wait(gx.at[m], g_sem.at[m])
        for k in range(SECTIONS):
            xd[slot, pl.ds(8 * k, 8), :] = gx[m, k]

    def send_chunk(slot, c0):
        for c in range(c0, c0 + CHUNK // PC):
            for h in range(ROWS // PR):
                q = c * (ROWS // PR) + h
                pltpu.make_async_remote_copy(
                    out.at[slot, pl.ds(h * PR, PR), pl.ds(c * PC, PC)],
                    p1[slot].at[r], p1_send.at[slot], p1_recv.at[slot],
                    device_id=dev(relay_at, q), device_id_type=MESH).start()

    def forward(m):
        @pl.when(t == 0)
        def _():
            assemble(m, m)

        @pl.when(t != 0)
        def _():
            wait(xd.at[m], p2_recv.at[m])

        af = xd[m].astype(F32)
        rinv = lax.rsqrt(jnp.mean(af * af, axis=-1, keepdims=True) + EPS)
        rinv_b[m] = jnp.broadcast_to(rinv, (ROWS, 128))
        nb = (af * rinv).astype(BF16)
        nbuf[m] = nb[:, :BUCKET]

        if m == 0:
            loads[0].wait()
            loads[1].wait()

        g = jnp.dot(nb, gate[...], preferred_element_type=F32)
        u = jnp.dot(nb, up[...], preferred_element_type=F32)
        sg = jax.nn.sigmoid(g)
        gs = g * sg
        hidden = (gs * u).astype(BF16)

        if m == 0:
            loads[2].wait()

        for c in range(0, D, CHUNK):
            res = xd[m, :, pl.ds(c, CHUNK)].astype(F32) + jnp.dot(
                hidden, down[:, pl.ds(c, CHUNK)], preferred_element_type=F32)
            out[m, :, pl.ds(c, CHUNK)] = res.astype(BF16)

            @pl.when(t < SECTIONS - 1)
            def _():
                send_chunk(m, c // PC)

        pltpu.make_async_copy(out.at[m], act_h.at[0, 0, m], o_sem).start()
        g_b[m] = g
        u_b[m] = u
        a_b[m] = u * sg * (1.0 + g * (1.0 - sg))
        b_b[m] = gs

    def backward(m):
        slot = MICRO + m

        @pl.when(t == SECTIONS - 1)
        def _():
            assemble(m, slot)

        @pl.when(t != SECTIONS - 1)
        def _():
            wait(xd.at[slot], p2_recv.at[slot])

        dout = xd[slot]
        dh = contract_last(dout, down[...])
        dg = (dh * a_b[m]).astype(BF16)
        du = (dh * b_b[m]).astype(BF16)
        both = dg.astype(F32) * g_b[m] + du.astype(F32) * u_b[m]
        corr = jnp.sum(both, axis=-1, keepdims=True) * (1.0 / D)
        rinv = rinv_b[m][:, :1]
        for c in range(0, D, CHUNK):
            dn = contract_last(dg, gate[pl.ds(c, CHUNK), :]) + contract_last(du, up[pl.ds(c, CHUNK), :])
            n = xd[m, :, pl.ds(c, CHUNK)].astype(F32) * rinv
            res = xd[slot, :, pl.ds(c, CHUNK)].astype(F32) + rinv * (dn - n * corr)
            out[slot, :, pl.ds(c, CHUNK)] = res.astype(BF16)

            @pl.when(t > 0)
            def _():
                send_chunk(slot, c // PC)

        pltpu.make_async_copy(out.at[slot], ig_h.at[0, 0, m], o_sem).start()
        part = lax.dot_general(nbuf[m], dg, (((0,), (0,)), ((), ())), preferred_element_type=F32)

        total[...] = part if m == 0 else total[...] + part

    half = lax.rem(r, ROWS // PR)
    col = r // (ROWS // PR)

    def relay(slot, goal, index):
        wait(p1[slot], p1_recv.at[slot])
        place = xd.at[slot, pl.ds(pl.multiple_of(half * PR, PR), PR), pl.ds(pl.multiple_of(col * PC, PC), PC)]

        def body(d, carry):
            snd[slot, d] = p1[slot][index(d)]
            pltpu.make_async_remote_copy(
                snd.at[slot, d], place, p2_send.at[slot], p2_recv.at[slot],
                device_id=dev(goal, d), device_id_type=MESH).start()
            return carry

        lax.fori_loop(0, REPLICAS, body, 0)

    def relay_forward():
        @pl.when(source < SECTIONS - 1)
        def _():
            for m in range(MICRO):
                relay(m, source + 1, lambda d: inv_s[m, d, 0])

    def relay_backward():
        @pl.when(source > 0)
        def _():
            for m in range(MICRO):
                relay(MICRO + m, source - 1, lambda d: routes_s[source - 1, m, d])

        @pl.when(r < BP)
        def _():
            slot = 2 * MICRO
            wait(p1[slot], p1_recv.at[slot])
            brow, bcol = r // (FF // PC), lax.rem(r, FF // PC)
            place = partner.at[pl.ds(pl.multiple_of(brow * PR, PR), PR), pl.ds(pl.multiple_of(bcol * PC, PC), PC)]

            def body(d, carry):
                snd[slot, d] = p1[slot][pairing_s[source, d]]
                pltpu.make_async_remote_copy(
                    snd.at[slot, d], place, p2_send.at[slot], p2_recv.at[slot],
                    device_id=dev(source, d), device_id_type=MESH).start()
                return carry

            lax.fori_loop(0, REPLICAS, body, 0)

    early = t < SECTIONS // 2

    @pl.when(jnp.logical_not(early))
    def _():
        relay_forward()

    for m in range(MICRO):
        forward(m)

    @pl.when(early)
    def _():
        relay_forward()
        relay_backward()

    for m in range(MICRO):
        backward(m)

    wait(mom, m_sem)
    fresh[...] = (BETA * mom[...] + (1.0 - BETA) * total[...]).astype(BF16)
    for q in range(BP):
        pltpu.make_async_remote_copy(
            fresh.at[pl.ds(q // (FF // PC) * PR, PR), pl.ds(q % (FF // PC) * PC, PC)],
            p1[2 * MICRO].at[r], p1_send.at[2 * MICRO], p1_recv.at[2 * MICRO],
            device_id=dev(relay_at, q), device_id_type=MESH).start()

    @pl.when(jnp.logical_not(early))
    def _():
        relay_backward()

    wait(partner, p2_recv.at[2 * MICRO])
    bucket[...] = 0.5 * (fresh[...].astype(F32) + partner[...].astype(F32))
    pltpu.make_async_copy(bucket, buck_h.at[0, 0], m_sem).start()

    wait(fresh, p1_send.at[2 * MICRO])

    @pl.when(r < BP)
    def _():
        wait(snd.at[2 * MICRO], p2_send.at[2 * MICRO])

    @pl.when(t < SECTIONS - 1)
    def _():
        for m in range(MICRO):
            wait(out.at[m], p1_send.at[m])

    @pl.when(t > 0)
    def _():
        for m in range(MICRO):
            wait(out.at[MICRO + m], p1_send.at[MICRO + m])

    @pl.when(source < SECTIONS - 1)
    def _():
        for m in range(MICRO):
            wait(snd.at[m], p2_send.at[m])

    @pl.when(source > 0)
    def _():
        for m in range(MICRO):
            wait(snd.at[MICRO + m], p2_send.at[MICRO + m])

    def sent(src, sems):
        for m in range(MICRO):
            pltpu.make_async_remote_copy(
                src.at[0, m], gx.at[m, t], gs_sem.at[sems + m], g_sem.at[m],
                device_id=dev(0, r), device_id_type=MESH).wait_send()

    @pl.when(t != 0)
    def _():
        sent(inp, 0)

    @pl.when(t != SECTIONS - 1)
    def _():
        sent(cot, MICRO)

    wait(out, o_sem)
    wait(bucket, m_sem)


def local(inputs, cotangent, gate_weight, up_weight, down_weight, momentum, routes, pairing):
    hbm = pl.BlockSpec(memory_space=pl.ANY)
    smem = pl.BlockSpec(memory_space=pltpu.SMEM)
    vmem = pl.BlockSpec(memory_space=pltpu.VMEM)
    dma = pltpu.SemaphoreType.DMA
    slots = 2 * MICRO
    return pl.pallas_call(
        kernel,
        out_shape=(
            jax.ShapeDtypeStruct((1, 1, MICRO, ROWS, D), BF16),
            jax.ShapeDtypeStruct((1, 1, MICRO, ROWS, D), BF16),
            jax.ShapeDtypeStruct((1, 1, BUCKET, FF), F32),
        ),
        in_specs=[hbm] * 6 + [vmem, smem, smem],
        out_specs=(hbm, hbm, hbm),
        scratch_shapes=[
            pltpu.VMEM((D, FF), BF16),
            pltpu.VMEM((D, FF), BF16),
            pltpu.VMEM((FF, D), BF16),
            pltpu.VMEM((BUCKET, FF), F32),
            pltpu.VMEM((MICRO, SECTIONS, ROWS // SECTIONS, D), BF16),
            pltpu.VMEM((slots, ROWS, D), BF16),
            pltpu.VMEM((slots, ROWS, D), BF16),
            *[pltpu.VMEM((REPLICAS, PR, PC), BF16)] * (slots + 1),
            pltpu.VMEM((slots + 1, REPLICAS, PR, PC), BF16),
            pltpu.VMEM((MICRO, ROWS, BUCKET), BF16),
            pltpu.VMEM((MICRO, ROWS, 128), F32),
            pltpu.VMEM((MICRO, ROWS, FF), F32),
            pltpu.VMEM((MICRO, ROWS, FF), F32),
            pltpu.VMEM((MICRO, ROWS, FF), F32),
            pltpu.VMEM((MICRO, ROWS, FF), F32),
            pltpu.VMEM((BUCKET, FF), F32),
            pltpu.VMEM((BUCKET, FF), BF16),
            pltpu.VMEM((BUCKET, FF), BF16),
            pltpu.VMEM((BUCKET, FF), F32),
            pltpu.VMEM((MICRO, REPLICAS, 128), jnp.int32),
            pltpu.SMEM((MICRO, REPLICAS, 128), jnp.int32),
            dma((3,)),
            dma,
            dma((MICRO,)),
            dma((2 * MICRO,)),
            dma((slots + 1,)),
            dma((slots + 1,)),
            dma((slots + 1,)),
            dma((slots + 1,)),
            dma,
            dma,
        ],
        compiler_params=pltpu.CompilerParams(has_side_effects=True, vmem_limit_bytes=56 << 20),
    )(inputs, cotangent, gate_weight, up_weight, down_weight, momentum, routes, routes, pairing)


def solution(mesh):
    placed = (
        P("replica", None, "section", None),
        P("replica", None, "section", None),
        P("section", "replica", None, None),
        P("section", "replica", None, None),
        P("section", "replica", None, None),
        P("section", "replica", None, None),
        P(),
        P(),
    )
    return jax.shard_map(
        local,
        mesh=mesh,
        in_specs=placed,
        out_specs=(
            P("section", "replica", None, None, None),
            P("section", "replica", None, None, None),
            P("section", "replica", None, None),
        ),
        check_vma=False,
    )
```

time: 1160 us -> 352 us (0.30)
  waiting for transfers between devices: 594 us -> 0 us
  Pallas kernels: 0 us -> 345 us
  starting transfers between devices: 320 us -> 0 us
  local copies, waits for them, and re-layouts: 80.2 us -> 5.53 us
  blocking collectives: 66.6 us -> 0 us
  other arithmetic: 56.8 us -> 0 us
  matrix products: 30.9 us -> 0 us
    all_to_all x37 -> x0, waiting for transfers between devices: 374 us -> none  [the longest x18 187 us: route(): lax.all_to_all(ordered, 'replica', split_axis=0, concat_axis=0, tiled=True)]
    pallas_call x0 -> x1, Pallas kernels: none -> 345 us  [local(): pl.pallas_call(kernel, out_shape=(jax.ShapeDtypeStruct((1, 1, MICRO, ROWS...]
    all_to_all x37 -> x0, starting transfers between devices: 240 us -> none  [the longest x19 134 us: route(): lax.all_to_all(pieces, 'replica', split_axis=0, concat_axis=0, tiled=True)]
    ppermute x18 -> x0, waiting for transfers between devices: 221 us -> none  [passed_along(): return lax.ppermute(block, axis, route)]
    ppermute x18 -> x0, starting transfers between devices: 80.3 us -> none  [passed_along(): return lax.ppermute(block, axis, route)]
    all_gather x2 -> x0, blocking collectives: 51.6 us -> none  [the longest x1 26 us: local(): lax.all_gather(inputs[0], 'section', axis=1, tiled=True)]
    dot_general x16 -> x0, matrix products: 30.9 us -> none  [the longest x6 8.55 us: contract_last(): lax.dot_general(left, right, (((1,), (1,)), ((), ())), preferred_element_...]
    reshape x37 -> x0, local copies, waits for them, and re-layouts: 27.7 us -> none  [the longest x19 25.9 us: route(): pieces = block.reshape((count, block.shape[0] // count) + block.shape[1:])]
  transfers between devices with their start and end apart: 55 -> 0, of which waited for: 55 -> 0; matrix products, arithmetic and copies ran while one was open for 2% -> 0% of each run, Pallas kernels for 0% -> 0%
where the time goes in v1:
time: 352 us
  Pallas kernels  345 us (98%)
  local copies, waits for them, and re-layouts  5.53 us (2%)
    pallas_call x1, Pallas kernels, local(): pl.pallas_call(kernel, out_shape=(jax.ShapeDtypeStruct((1, 1, MICRO, ROWS...  345 us

profile of v1, /device:TPU:25, one launch (start us, length us, event | category | flops | bytes accessed | tf_op | source)
XLA Modules:
  0.0 351.5 jit_solution(2027127682056077635)
XLA Ops:
  0.6 345.3 %shard_map.103 = (bf16[1,1,2,64,2048]{4,3,2,1,0:T(8,128)(2,1)}, bf16[1,1,2,64,2048]{4,3,2,1,0:T(8,128)(2,1)}, f32[1,1,128,768]{3,2,1,0:T(8,128)}) custom-call(bf16[1,2,8,2048]{3,2,1,0:T(8,128)(2,1)} %inp.1, bf16[1,2,8,2048]{3,2,1,0:T(8,128)(2,1)} %cot.1, bf16[1,1,2048,768]{3,2,1,0:T(8,128)(2,1)} %gate_h.1, bf16[1,1,2048,768]{3,2,1,0:T(8,128)(2,1)} %up_h.1, ...), custom_call_target="tpu_custom_call" | custom-call | tf_op jit(solution)/shard_map/pallas_call | solution.py:289
  346.0 1.9 copy.14
  347.9 1.9 copy.15
  349.7 1.8 copy.16

commit v2 on v1

--- a/solution.py
+++ b/solution.py
@@ -12,29 +12,35 @@
 SECTIONS, REPLICAS, MICRO, ROWS, D, FF, BUCKET = 8, 32, 2, 64, 2048, 768, 128
 PR, PC = 32, 128
 CHUNK = 256
+GROUPS = 4
+SPAN = D // GROUPS
 BP = (BUCKET // PR) * (FF // PC)
-
-
-def contract_last(a, b):
-    return lax.dot_general(a, b, (((1,), (1,)), ((), ())), preferred_element_type=F32)
 
 
 def kernel(inp, cot, gate_h, up_h, down_h, mom_h, routes_v, routes_s, pairing_s,
            act_h, ig_h, buck_h,
            gate, up, down, mom, gx, xd, out, p1a, p1b, p1c, p1d, p1e, snd, nbuf, rinv_b, g_b, u_b, a_b, b_b, total,
            fresh, partner, bucket, inv_v, inv_s,
-           w_sem, m_sem, g_sem, gs_sem, p1_recv, p1_send, p2_recv, p2_send, o_sem, i_sem):
+           gate_t, up_t, down_t,
+           w_sem, m_sem, g_sem, gs_sem, p1_recv, p1_send, p2_recv, b_recv, p2_send, o_sem, i_sem):
     t = lax.axis_index("section")
     r = lax.axis_index("replica")
     p1 = (p1a, p1b, p1c, p1d, p1e)
-    relay_at = lax.rem(t + 4, SECTIONS)
-    source = lax.rem(t + 4, SECTIONS)
+    across = lax.rem(t + 4, SECTIONS)
+    core, ry, rz = lax.rem(r, 2), r // 8, lax.rem(r, 8) // 2
+    group = lax.rem(rz - ry + 4, 4)
+    half = lax.rem(ry, ROWS // PR)
+    col = 2 * (2 * group + core) + ry // (ROWS // PR)
+    fwd_source = lax.rem(t + 4 - core, SECTIONS)
+    bwd_source = lax.rem(t + 4 + core, SECTIONS)
 
     def dev(s, q):
         return {"section": s, "replica": q}
 
     def wait(ref, sem):
         pltpu.make_async_copy(ref, ref, sem).wait()
+
+    early = t < SECTIONS // 2
 
     loads = [pltpu.make_async_copy(h, v, w_sem.at[i])
              for i, (h, v) in enumerate(((gate_h.at[0, 0], gate), (up_h.at[0, 0], up), (down_h.at[0, 0], down)))]
@@ -58,7 +64,7 @@
     gather(cot, SECTIONS - 1, MICRO)
     pltpu.make_async_copy(mom_h.at[0, 0], mom, m_sem).start()
 
-    rv = routes_v[jnp.minimum(source, SECTIONS - 2)]
+    rv = routes_v[jnp.minimum(fwd_source, SECTIONS - 2)]
     goal_id = lax.broadcasted_iota(jnp.int32, (REPLICAS, REPLICAS), 0)
     from_id = lax.broadcasted_iota(jnp.int32, (REPLICAS, REPLICAS), 1)
     for m in range(MICRO):
@@ -74,42 +80,55 @@
         for k in range(SECTIONS):
             xd[slot, pl.ds(8 * k, 8), :] = gx[m, k]
 
-    def send_chunk(slot, c0):
-        for c in range(c0, c0 + CHUNK // PC):
-            for h in range(ROWS // PR):
-                q = c * (ROWS // PR) + h
-                pltpu.make_async_remote_copy(
-                    out.at[slot, pl.ds(h * PR, PR), pl.ds(c * PC, PC)],
-                    p1[slot].at[r], p1_send.at[slot], p1_recv.at[slot],
-                    device_id=dev(relay_at, q), device_id_type=MESH).start()
+    def send_chunk(slot, j):
+        step = 1 if slot < MICRO else -1
+        at = across if j % 2 == 0 else lax.rem(t + 4 + step, SECTIONS)
+        for k in range(4):
+            c, h = 2 * j + k // 2, k % 2
+            q = k * 8 + (j // 2 + k) % 4 * 2 + j % 2
+            pltpu.make_async_remote_copy(
+                out.at[slot, pl.ds(h * PR, PR), pl.ds(c * PC, PC)],
+                p1[slot].at[r], p1_send.at[slot], p1_recv.at[slot],
+                device_id=dev(at, q), device_id_type=MESH).start()
 
     def forward(m):
         @pl.when(t == 0)
         def _():
             assemble(m, m)
 
-        @pl.when(t != 0)
-        def _():
-            wait(xd.at[m], p2_recv.at[m])
-
-        af = xd[m].astype(F32)
-        rinv = lax.rsqrt(jnp.mean(af * af, axis=-1, keepdims=True) + EPS)
-        rinv_b[m] = jnp.broadcast_to(rinv, (ROWS, 128))
-        nb = (af * rinv).astype(BF16)
-        nbuf[m] = nb[:, :BUCKET]
-
         if m == 0:
-            loads[0].wait()
-            loads[1].wait()
-
-        g = jnp.dot(nb, gate[...], preferred_element_type=F32)
-        u = jnp.dot(nb, up[...], preferred_element_type=F32)
+            @pl.when(early)
+            def _():
+                loads[0].wait()
+                loads[1].wait()
+
+        squares = jnp.zeros((ROWS, 128), F32)
+        g = jnp.zeros((ROWS, FF), F32)
+        u = jnp.zeros((ROWS, FF), F32)
+        for k in range(GROUPS):
+            cols = pl.ds(k * SPAN, SPAN)
+
+            @pl.when(t != 0)
+            def _():
+                wait(xd.at[m, :, cols], p2_recv.at[m, k])
+
+            a = xd[m, :, cols]
+            g = g + jnp.dot(a, gate[cols, :], preferred_element_type=F32)
+            u = u + jnp.dot(a, up[cols, :], preferred_element_type=F32)
+            for c in range(0, SPAN, 128):
+                af = a[:, c:c + 128].astype(F32)
+                squares = squares + af * af
+        rinv = lax.rsqrt(jnp.sum(squares, axis=-1, keepdims=True) * (1.0 / D) + EPS)
+        g = g * rinv
+        u = u * rinv
         sg = jax.nn.sigmoid(g)
         gs = g * sg
         hidden = (gs * u).astype(BF16)
 
         if m == 0:
-            loads[2].wait()
+            @pl.when(early)
+            def _():
+                loads[2].wait()
 
         for c in range(0, D, CHUNK):
             res = xd[m, :, pl.ds(c, CHUNK)].astype(F32) + jnp.dot(
@@ -118,9 +137,11 @@
 
             @pl.when(t < SECTIONS - 1)
             def _():
-                send_chunk(m, c // PC)
+                send_chunk(m, c // CHUNK)
 
         pltpu.make_async_copy(out.at[m], act_h.at[0, 0, m], o_sem).start()
+        rinv_b[m] = jnp.broadcast_to(rinv, (ROWS, 128))
+        nbuf[m] = (xd[m, :, :BUCKET].astype(F32) * rinv).astype(BF16)
         g_b[m] = g
         u_b[m] = u
         a_b[m] = u * sg * (1.0 + g * (1.0 - sg))
@@ -133,34 +154,36 @@
         def _():
             assemble(m, slot)
 
-        @pl.when(t != SECTIONS - 1)
-        def _():
-            wait(xd.at[slot], p2_recv.at[slot])
-
-        dout = xd[slot]
-        dh = contract_last(dout, down[...])
+        dh = jnp.zeros((ROWS, FF), F32)
+        for k in range(GROUPS):
+            cols = pl.ds(k * SPAN, SPAN)
+
+            @pl.when(t != SECTIONS - 1)
+            def _():
+                wait(xd.at[slot, :, cols], p2_recv.at[slot, k])
+
+            dh = dh + jnp.dot(xd[slot, :, cols], down_t[cols, :], preferred_element_type=F32)
         dg = (dh * a_b[m]).astype(BF16)
         du = (dh * b_b[m]).astype(BF16)
         both = dg.astype(F32) * g_b[m] + du.astype(F32) * u_b[m]
         corr = jnp.sum(both, axis=-1, keepdims=True) * (1.0 / D)
         rinv = rinv_b[m][:, :1]
         for c in range(0, D, CHUNK):
-            dn = contract_last(dg, gate[pl.ds(c, CHUNK), :]) + contract_last(du, up[pl.ds(c, CHUNK), :])
+            cols = pl.ds(c, CHUNK)
+            dn = jnp.dot(dg, gate_t[:, cols], preferred_element_type=F32) + jnp.dot(
+                du, up_t[:, cols], preferred_element_type=F32)
             n = xd[m, :, pl.ds(c, CHUNK)].astype(F32) * rinv
             res = xd[slot, :, pl.ds(c, CHUNK)].astype(F32) + rinv * (dn - n * corr)
             out[slot, :, pl.ds(c, CHUNK)] = res.astype(BF16)
 
             @pl.when(t > 0)
             def _():
-                send_chunk(slot, c // PC)
+                send_chunk(slot, c // CHUNK)
 
         pltpu.make_async_copy(out.at[slot], ig_h.at[0, 0, m], o_sem).start()
         part = lax.dot_general(nbuf[m], dg, (((0,), (0,)), ((), ())), preferred_element_type=F32)
 
         total[...] = part if m == 0 else total[...] + part
-
-    half = lax.rem(r, ROWS // PR)
-    col = r // (ROWS // PR)
 
     def relay(slot, goal, index):
         wait(p1[slot], p1_recv.at[slot])
@@ -169,24 +192,25 @@
         def body(d, carry):
             snd[slot, d] = p1[slot][index(d)]
             pltpu.make_async_remote_copy(
-                snd.at[slot, d], place, p2_send.at[slot], p2_recv.at[slot],
+                snd.at[slot, d], place, p2_send.at[slot], p2_recv.at[slot, group],
                 device_id=dev(goal, d), device_id_type=MESH).start()
             return carry
 
-        lax.fori_loop(0, REPLICAS, body, 0)
+        lax.fori_loop(0, REPLICAS, body, 0, unroll=4)
 
     def relay_forward():
-        @pl.when(source < SECTIONS - 1)
+        @pl.when(fwd_source < SECTIONS - 1)
         def _():
             for m in range(MICRO):
-                relay(m, source + 1, lambda d: inv_s[m, d, 0])
+                relay(m, fwd_source + 1, lambda d: inv_s[m, d, 0])
 
     def relay_backward():
-        @pl.when(source > 0)
+        @pl.when(bwd_source > 0)
         def _():
             for m in range(MICRO):
-                relay(MICRO + m, source - 1, lambda d: routes_s[source - 1, m, d])
-
+                relay(MICRO + m, bwd_source - 1, lambda d: routes_s[bwd_source - 1, m, d])
+
+    def relay_bucket():
         @pl.when(r < BP)
         def _():
             slot = 2 * MICRO
@@ -195,27 +219,40 @@
             place = partner.at[pl.ds(pl.multiple_of(brow * PR, PR), PR), pl.ds(pl.multiple_of(bcol * PC, PC), PC)]
 
             def body(d, carry):
-                snd[slot, d] = p1[slot][pairing_s[source, d]]
+                snd[slot, d] = p1[slot][pairing_s[across, d]]
                 pltpu.make_async_remote_copy(
-                    snd.at[slot, d], place, p2_send.at[slot], p2_recv.at[slot],
-                    device_id=dev(source, d), device_id_type=MESH).start()
+                    snd.at[slot, d], place, p2_send.at[slot], b_recv,
+                    device_id=dev(across, d), device_id_type=MESH).start()
                 return carry
 
             lax.fori_loop(0, REPLICAS, body, 0)
 
-    early = t < SECTIONS // 2
+    def transpose():
+        def body(i, carry):
+            cols = pl.ds(pl.multiple_of(i * CHUNK, CHUNK), CHUNK)
+            gate_t[:, cols] = gate[cols, :].T
+            up_t[:, cols] = up[cols, :].T
+            down_t[cols, :] = down[:, cols].T
+            return carry
+
+        lax.fori_loop(0, D // CHUNK, body, 0)
 
     @pl.when(jnp.logical_not(early))
     def _():
         relay_forward()
+        for load in loads:
+            load.wait()
+        transpose()
 
     for m in range(MICRO):
         forward(m)
 
     @pl.when(early)
     def _():
+        transpose()
         relay_forward()
         relay_backward()
+        relay_bucket()
 
     for m in range(MICRO):
         backward(m)
@@ -226,13 +263,14 @@
         pltpu.make_async_remote_copy(
             fresh.at[pl.ds(q // (FF // PC) * PR, PR), pl.ds(q % (FF // PC) * PC, PC)],
             p1[2 * MICRO].at[r], p1_send.at[2 * MICRO], p1_recv.at[2 * MICRO],
-            device_id=dev(relay_at, q), device_id_type=MESH).start()
+            device_id=dev(across, q), device_id_type=MESH).start()
 
     @pl.when(jnp.logical_not(early))
     def _():
         relay_backward()
-
-    wait(partner, p2_recv.at[2 * MICRO])
+        relay_bucket()
+
+    wait(partner, b_recv)
     bucket[...] = 0.5 * (fresh[...].astype(F32) + partner[...].astype(F32))
     pltpu.make_async_copy(bucket, buck_h.at[0, 0], m_sem).start()
 
@@ -252,12 +290,12 @@
         for m in range(MICRO):
             wait(out.at[MICRO + m], p1_send.at[MICRO + m])
 
-    @pl.when(source < SECTIONS - 1)
+    @pl.when(fwd_source < SECTIONS - 1)
     def _():
         for m in range(MICRO):
             wait(snd.at[m], p2_send.at[m])
 
-    @pl.when(source > 0)
+    @pl.when(bwd_source > 0)
     def _():
         for m in range(MICRO):
             wait(snd.at[MICRO + m], p2_send.at[MICRO + m])
@@ -278,6 +316,19 @@
 
     wait(out, o_sem)
     wait(bucket, m_sem)
+
+
+def hand_over(*refs):
+    came, made, held, sem = refs[:3], refs[3:6], refs[6:9], refs[9]
+    into = [pltpu.make_async_copy(came[i], held[i], sem.at[i]) for i in range(3)]
+    away = [pltpu.make_async_copy(held[i], made[i], sem.at[3 + i]) for i in range(3)]
+    for copy in into:
+        copy.start()
+    for i in range(3):
+        into[i].wait()
+        away[i].start()
+    for copy in away:
+        copy.wait()
 
 
 def local(inputs, cotangent, gate_weight, up_weight, down_weight, momentum, routes, pairing):
@@ -286,7 +337,7 @@
     vmem = pl.BlockSpec(memory_space=pltpu.VMEM)
     dma = pltpu.SemaphoreType.DMA
     slots = 2 * MICRO
-    return pl.pallas_call(
+    made = pl.pallas_call(
         kernel,
         out_shape=(
             jax.ShapeDtypeStruct((1, 1, MICRO, ROWS, D), BF16),
@@ -317,19 +368,30 @@
             pltpu.VMEM((BUCKET, FF), F32),
             pltpu.VMEM((MICRO, REPLICAS, 128), jnp.int32),
             pltpu.SMEM((MICRO, REPLICAS, 128), jnp.int32),
+            pltpu.VMEM((FF, D), BF16),
+            pltpu.VMEM((FF, D), BF16),
+            pltpu.VMEM((D, FF), BF16),
             dma((3,)),
             dma,
             dma((MICRO,)),
             dma((2 * MICRO,)),
             dma((slots + 1,)),
             dma((slots + 1,)),
-            dma((slots + 1,)),
+            dma((slots, GROUPS)),
+            dma,
             dma((slots + 1,)),
             dma,
             dma,
         ],
         compiler_params=pltpu.CompilerParams(has_side_effects=True, vmem_limit_bytes=56 << 20),
     )(inputs, cotangent, gate_weight, up_weight, down_weight, momentum, routes, routes, pairing)
+    return pl.pallas_call(
+        hand_over,
+        out_shape=tuple(jax.ShapeDtypeStruct(a.shape, a.dtype) for a in made),
+        in_specs=[hbm] * 3,
+        out_specs=(hbm, hbm, hbm),
+        scratch_shapes=[*[pltpu.VMEM(a.shape, a.dtype) for a in made], dma((6,))],
+    )(*made)
 
 
 def solution(mesh):

time: 352 us -> 308 us (0.88)
  Pallas kernels: 345 us -> 308 us
  local copies, waits for them, and re-layouts: 5.53 us -> 0 us
    pallas_call x1, Pallas kernels: 345 us -> 305 us  [local(): pl.pallas_call(kernel, out_shape=(jax.ShapeDtypeStruct((1, 1, MICRO, ROWS...]
    unnamed x3 -> x0, local copies, waits for them, and re-layouts: 5.53 us -> none
where the time goes in v2:
time: 308 us
  Pallas kernels  308 us (100%)
    pallas_call x1, Pallas kernels, local(): pl.pallas_call(kernel, out_shape=(jax.ShapeDtypeStruct((1, 1, MICRO, ROWS...  305 us

profile of v2, /device:TPU:25, one launch (start us, length us, event | category | flops | bytes accessed | tf_op | source)
XLA Modules:
  0.0 308.3 jit_solution(14915228762516533865)
XLA Ops:
  0.6 305.5 %shard_map.103 = (bf16[1,1,2,64,2048]{4,3,2,1,0:T(8,128)(2,1)}, bf16[1,1,2,64,2048]{4,3,2,1,0:T(8,128)(2,1)}, f32[1,1,128,768]{3,2,1,0:T(8,128)}) custom-call(bf16[1,2,8,2048]{3,2,1,0:T(8,128)(2,1)} %inp.1, bf16[1,2,8,2048]{3,2,1,0:T(8,128)(2,1)} %cot.1, bf16[1,1,2048,768]{3,2,1,0:T(8,128)(2,1)} %gate_h.1, bf16[1,1,2048,768]{3,2,1,0:T(8,128)(2,1)} %up_h.1, ...), custom_call_target="tpu_custom_call" | custom-call | tf_op jit(solution)/shard_map/pallas_call | solution.py:340
  306.1 2.2 shard_map.104

commit v3 on v2

--- a/solution.py
+++ b/solution.py
@@ -10,27 +10,29 @@
 MESH = pl.DeviceIdType.MESH
 F32, BF16 = jnp.float32, jnp.bfloat16
 SECTIONS, REPLICAS, MICRO, ROWS, D, FF, BUCKET = 8, 32, 2, 64, 2048, 768, 128
-PR, PC = 32, 128
+UNITS = 4
+UROWS = MICRO * ROWS // UNITS
+PR, PC = UROWS // 2, 128
+BR, BC = 32, 128
 CHUNK = 256
 GROUPS = 4
 SPAN = D // GROUPS
-BP = (BUCKET // PR) * (FF // PC)
+BP = (BUCKET // BR) * (FF // BC)
 
 
 def kernel(inp, cot, gate_h, up_h, down_h, mom_h, routes_v, routes_s, pairing_s,
            act_h, ig_h, buck_h,
-           gate, up, down, mom, gx, xd, out, p1a, p1b, p1c, p1d, p1e, snd, nbuf, rinv_b, g_b, u_b, a_b, b_b, total,
+           gate, up, down, mom, gx, xd, out, p1, sel, snd, pb, snb, nbuf, rinv_b, g_b, u_b, a_b, b_b, total,
            fresh, partner, bucket, inv_v, inv_s,
            gate_t, up_t, down_t,
-           w_sem, m_sem, g_sem, gs_sem, p1_recv, p1_send, p2_recv, b_recv, p2_send, o_sem, i_sem):
+           w_sem, m_sem, g_sem, gs_sem, p1_recv, p1_send, p2_recv, p2_send, pb_recv, pb_send, b_recv, snb_send, o_sem, i_sem):
     t = lax.axis_index("section")
     r = lax.axis_index("replica")
-    p1 = (p1a, p1b, p1c, p1d, p1e)
     across = lax.rem(t + 4, SECTIONS)
     core, ry, rz = lax.rem(r, 2), r // 8, lax.rem(r, 8) // 2
     group = lax.rem(rz - ry + 4, 4)
-    half = lax.rem(ry, ROWS // PR)
-    col = 2 * (2 * group + core) + ry // (ROWS // PR)
+    half = lax.rem(ry, 2)
+    col = 2 * (2 * group + core) + ry // 2
     fwd_source = lax.rem(t + 4 - core, SECTIONS)
     bwd_source = lax.rem(t + 4 + core, SECTIONS)
 
@@ -45,17 +47,21 @@
     loads = [pltpu.make_async_copy(h, v, w_sem.at[i])
              for i, (h, v) in enumerate(((gate_h.at[0, 0], gate), (up_h.at[0, 0], up), (down_h.at[0, 0], down)))]
 
+    per = SECTIONS * MICRO // UNITS
+
     def gather(src, goal, sems):
-        @pl.when(t == goal)
-        def _():
-            for m in range(MICRO):
-                pltpu.make_async_copy(src.at[0, m], gx.at[m, t], g_sem.at[m]).start()
-
-        @pl.when(t != goal)
-        def _():
-            for m in range(MICRO):
+        for m in range(MICRO):
+            unit = m * (UNITS // MICRO) + t // per
+            place = gx.at[unit, lax.rem(t, per)]
+
+            @pl.when(t == goal)
+            def _():
+                pltpu.make_async_copy(src.at[0, m], place, g_sem.at[unit]).start()
+
+            @pl.when(t != goal)
+            def _():
                 pltpu.make_async_remote_copy(
-                    src.at[0, m], gx.at[m, t], gs_sem.at[sems + m], g_sem.at[m],
+                    src.at[0, m], place, gs_sem.at[sems + m], g_sem.at[unit],
                     device_id=dev(goal, r), device_id_type=MESH).start()
 
     gather(inp, 0, 0)
@@ -77,34 +83,35 @@
 
     def assemble(m, slot):
         wait(gx.at[m], g_sem.at[m])
-        for k in range(SECTIONS):
+        for k in range(per):
             xd[slot, pl.ds(8 * k, 8), :] = gx[m, k]
 
-    def send_chunk(slot, j):
-        step = 1 if slot < MICRO else -1
+    def send_chunk(slot, j, step):
         at = across if j % 2 == 0 else lax.rem(t + 4 + step, SECTIONS)
         for k in range(4):
             c, h = 2 * j + k // 2, k % 2
             q = k * 8 + (j // 2 + k) % 4 * 2 + j % 2
             pltpu.make_async_remote_copy(
                 out.at[slot, pl.ds(h * PR, PR), pl.ds(c * PC, PC)],
-                p1[slot].at[r], p1_send.at[slot], p1_recv.at[slot],
+                p1.at[slot, r], p1_send.at[slot], p1_recv.at[slot],
                 device_id=dev(at, q), device_id_type=MESH).start()
+
+    def rows_of(m):
+        return pl.ds(pl.multiple_of(lax.rem(m, 2) * UROWS, UROWS), UROWS)
 
     def forward(m):
         @pl.when(t == 0)
         def _():
             assemble(m, m)
 
-        if m == 0:
-            @pl.when(early)
-            def _():
-                loads[0].wait()
-                loads[1].wait()
-
-        squares = jnp.zeros((ROWS, 128), F32)
-        g = jnp.zeros((ROWS, FF), F32)
-        u = jnp.zeros((ROWS, FF), F32)
+        @pl.when(jnp.logical_and(m == 0, early))
+        def _():
+            loads[0].wait()
+            loads[1].wait()
+
+        squares = jnp.zeros((UROWS, 128), F32)
+        g = jnp.zeros((UROWS, FF), F32)
+        u = jnp.zeros((UROWS, FF), F32)
         for k in range(GROUPS):
             cols = pl.ds(k * SPAN, SPAN)
 
@@ -125,10 +132,9 @@
         gs = g * sg
         hidden = (gs * u).astype(BF16)
 
-        if m == 0:
-            @pl.when(early)
-            def _():
-                loads[2].wait()
+        @pl.when(jnp.logical_and(m == 0, early))
+        def _():
+            loads[2].wait()
 
         for c in range(0, D, CHUNK):
             res = xd[m, :, pl.ds(c, CHUNK)].astype(F32) + jnp.dot(
@@ -137,10 +143,10 @@
 
             @pl.when(t < SECTIONS - 1)
             def _():
-                send_chunk(m, c // CHUNK)
-
-        pltpu.make_async_copy(out.at[m], act_h.at[0, 0, m], o_sem).start()
-        rinv_b[m] = jnp.broadcast_to(rinv, (ROWS, 128))
+                send_chunk(m, c // CHUNK, 1)
+
+        pltpu.make_async_copy(out.at[m], act_h.at[0, 0, m // 2, rows_of(m), :], o_sem).start()
+        rinv_b[m] = jnp.broadcast_to(rinv, (UROWS, 128))
         nbuf[m] = (xd[m, :, :BUCKET].astype(F32) * rinv).astype(BF16)
         g_b[m] = g
         u_b[m] = u
@@ -148,13 +154,13 @@
         b_b[m] = gs
 
     def backward(m):
-        slot = MICRO + m
+        slot = UNITS + m
 
         @pl.when(t == SECTIONS - 1)
         def _():
             assemble(m, slot)
 
-        dh = jnp.zeros((ROWS, FF), F32)
+        dh = jnp.zeros((UROWS, FF), F32)
         for k in range(GROUPS):
             cols = pl.ds(k * SPAN, SPAN)
 
@@ -178,54 +184,59 @@
 
             @pl.when(t > 0)
             def _():
-                send_chunk(slot, c // CHUNK)
-
-        pltpu.make_async_copy(out.at[slot], ig_h.at[0, 0, m], o_sem).start()
+                send_chunk(slot, c // CHUNK, -1)
+
+        pltpu.make_async_copy(out.at[slot], ig_h.at[0, 0, m // 2, rows_of(m), :], o_sem).start()
         part = lax.dot_general(nbuf[m], dg, (((0,), (0,)), ((), ())), preferred_element_type=F32)
 
-        total[...] = part if m == 0 else total[...] + part
+        total[...] = total[...] + part
 
     def relay(slot, goal, index):
-        wait(p1[slot], p1_recv.at[slot])
+        wait(p1.at[slot], p1_recv.at[slot])
+        sel[...] = p1[slot]
         place = xd.at[slot, pl.ds(pl.multiple_of(half * PR, PR), PR), pl.ds(pl.multiple_of(col * PC, PC), PC)]
 
         def body(d, carry):
-            snd[slot, d] = p1[slot][index(d)]
+            snd[slot, d] = sel[index(d)]
             pltpu.make_async_remote_copy(
                 snd.at[slot, d], place, p2_send.at[slot], p2_recv.at[slot, group],
                 device_id=dev(goal, d), device_id_type=MESH).start()
             return carry
 
-        lax.fori_loop(0, REPLICAS, body, 0, unroll=4)
+        lax.fori_loop(0, REPLICAS, body, 0, unroll=8)
+
+    def loop(body):
+        def step(m, carry):
+            body(m)
+            return carry
+
+        lax.fori_loop(0, UNITS, step, 0)
 
     def relay_forward():
         @pl.when(fwd_source < SECTIONS - 1)
         def _():
-            for m in range(MICRO):
-                relay(m, fwd_source + 1, lambda d: inv_s[m, d, 0])
+            loop(lambda m: relay(m, fwd_source + 1, lambda d: inv_s[m // 2, d, 0]))
 
     def relay_backward():
         @pl.when(bwd_source > 0)
         def _():
-            for m in range(MICRO):
-                relay(MICRO + m, bwd_source - 1, lambda d: routes_s[bwd_source - 1, m, d])
+            loop(lambda m: relay(UNITS + m, bwd_source - 1, lambda d: routes_s[bwd_source - 1, m // 2, d]))
 
     def relay_bucket():
         @pl.when(r < BP)
         def _():
-            slot = 2 * MICRO
-            wait(p1[slot], p1_recv.at[slot])
-            brow, bcol = r // (FF // PC), lax.rem(r, FF // PC)
-            place = partner.at[pl.ds(pl.multiple_of(brow * PR, PR), PR), pl.ds(pl.multiple_of(bcol * PC, PC), PC)]
+            wait(pb, pb_recv)
+            brow, bcol = r // (FF // BC), lax.rem(r, FF // BC)
+            place = partner.at[pl.ds(pl.multiple_of(brow * BR, BR), BR), pl.ds(pl.multiple_of(bcol * BC, BC), BC)]
 
             def body(d, carry):
-                snd[slot, d] = p1[slot][pairing_s[across, d]]
+                snb[d] = pb[pairing_s[across, d]]
                 pltpu.make_async_remote_copy(
-                    snd.at[slot, d], place, p2_send.at[slot], b_recv,
+                    snb.at[d], place, snb_send, b_recv,
                     device_id=dev(across, d), device_id_type=MESH).start()
                 return carry
 
-            lax.fori_loop(0, REPLICAS, body, 0)
+            lax.fori_loop(0, REPLICAS, body, 0, unroll=4)
 
     def transpose():
         def body(i, carry):
@@ -237,6 +248,8 @@
 
         lax.fori_loop(0, D // CHUNK, body, 0)
 
+    total[...] = jnp.zeros_like(total)
+
     @pl.when(jnp.logical_not(early))
     def _():
         relay_forward()
@@ -244,25 +257,37 @@
             load.wait()
         transpose()
 
-    for m in range(MICRO):
-        forward(m)
-
-    @pl.when(early)
-    def _():
-        transpose()
-        relay_forward()
-        relay_backward()
-        relay_bucket()
-
-    for m in range(MICRO):
-        backward(m)
+    last = t == SECTIONS - 1
+
+    def step(i, carry):
+        ahead = jnp.where(last, lax.rem(i, 2) == 0, i < UNITS)
+        m = jnp.where(last, i // 2, lax.rem(i, UNITS))
+
+        @pl.when(jnp.logical_and(i == UNITS, early))
+        def _():
+            transpose()
+            relay_forward()
+            relay_backward()
+            relay_bucket()
+
+        @pl.when(ahead)
+        def _():
+            forward(m)
+
+        @pl.when(jnp.logical_not(ahead))
+        def _():
+            backward(m)
+
+        return carry
+
+    lax.fori_loop(0, 2 * UNITS, step, 0)
 
     wait(mom, m_sem)
     fresh[...] = (BETA * mom[...] + (1.0 - BETA) * total[...]).astype(BF16)
     for q in range(BP):
         pltpu.make_async_remote_copy(
-            fresh.at[pl.ds(q // (FF // PC) * PR, PR), pl.ds(q % (FF // PC) * PC, PC)],
-            p1[2 * MICRO].at[r], p1_send.at[2 * MICRO], p1_recv.at[2 * MICRO],
+            fresh.at[pl.ds(q // (FF // BC) * BR, BR), pl.ds(q % (FF // BC) * BC, BC)],
+            pb.at[r], pb_send, pb_recv,
             device_id=dev(across, q), device_id_type=MESH).start()
 
     @pl.when(jnp.logical_not(early))
@@ -274,36 +299,32 @@
     bucket[...] = 0.5 * (fresh[...].astype(F32) + partner[...].astype(F32))
     pltpu.make_async_copy(bucket, buck_h.at[0, 0], m_sem).start()
 
-    wait(fresh, p1_send.at[2 * MICRO])
+    wait(fresh, pb_send)
 
     @pl.when(r < BP)
     def _():
-        wait(snd.at[2 * MICRO], p2_send.at[2 * MICRO])
+        wait(snb, snb_send)
 
     @pl.when(t < SECTIONS - 1)
     def _():
-        for m in range(MICRO):
-            wait(out.at[m], p1_send.at[m])
+        loop(lambda m: wait(out.at[m], p1_send.at[m]))
 
     @pl.when(t > 0)
     def _():
-        for m in range(MICRO):
-            wait(out.at[MICRO + m], p1_send.at[MICRO + m])
+        loop(lambda m: wait(out.at[UNITS + m], p1_send.at[UNITS + m]))
 
     @pl.when(fwd_source < SECTIONS - 1)
     def _():
-        for m in range(MICRO):
-            wait(snd.at[m], p2_send.at[m])
+        loop(lambda m: wait(snd.at[m], p2_send.at[m]))
 
     @pl.when(bwd_source > 0)
     def _():
-        for m in range(MICRO):
-            wait(snd.at[MICRO + m], p2_send.at[MICRO + m])
+        loop(lambda m: wait(snd.at[UNITS + m], p2_send.at[UNITS + m]))
 
     def sent(src, sems):
         for m in range(MICRO):
             pltpu.make_async_remote_copy(
-                src.at[0, m], gx.at[m, t], gs_sem.at[sems + m], g_sem.at[m],
+                src.at[0, m], gx.at[0, 0], gs_sem.at[sems + m], g_sem.at[0],
                 device_id=dev(0, r), device_id_type=MESH).wait_send()
 
     @pl.when(t != 0)
@@ -336,7 +357,7 @@
     smem = pl.BlockSpec(memory_space=pltpu.SMEM)
     vmem = pl.BlockSpec(memory_space=pltpu.VMEM)
     dma = pltpu.SemaphoreType.DMA
-    slots = 2 * MICRO
+    slots = 2 * UNITS
     made = pl.pallas_call(
         kernel,
         out_shape=(
@@ -351,17 +372,17 @@
             pltpu.VMEM((D, FF), BF16),
             pltpu.VMEM((FF, D), BF16),
             pltpu.VMEM((BUCKET, FF), F32),
-            pltpu.VMEM((MICRO, SECTIONS, ROWS // SECTIONS, D), BF16),
-            pltpu.VMEM((slots, ROWS, D), BF16),
-            pltpu.VMEM((slots, ROWS, D), BF16),
-            *[pltpu.VMEM((REPLICAS, PR, PC), BF16)] * (slots + 1),
-            pltpu.VMEM((slots + 1, REPLICAS, PR, PC), BF16),
-            pltpu.VMEM((MICRO, ROWS, BUCKET), BF16),
-            pltpu.VMEM((MICRO, ROWS, 128), F32),
-            pltpu.VMEM((MICRO, ROWS, FF), F32),
-            pltpu.VMEM((MICRO, ROWS, FF), F32),
-            pltpu.VMEM((MICRO, ROWS, FF), F32),
-            pltpu.VMEM((MICRO, ROWS, FF), F32),
+            pltpu.VMEM((UNITS, SECTIONS * MICRO // UNITS, ROWS // SECTIONS, D), BF16),
+            pltpu.VMEM((slots, UROWS, D), BF16),
+            pltpu.VMEM((slots, UROWS, D), BF16),
+            pltpu.VMEM((slots, REPLICAS, PR, PC), BF16),
+            pltpu.VMEM((REPLICAS, PR, PC), BF16),
+            pltpu.VMEM((slots, REPLICAS, PR, PC), BF16),
+            pltpu.VMEM((REPLICAS, BR, BC), BF16),
+            pltpu.VMEM((REPLICAS, BR, BC), BF16),
+            pltpu.VMEM((UNITS, UROWS, BUCKET), BF16),
+            pltpu.VMEM((UNITS, UROWS, 128), F32),
+            *[pltpu.VMEM((UNITS, UROWS, FF), F32)] * 4,
             pltpu.VMEM((BUCKET, FF), F32),
             pltpu.VMEM((BUCKET, FF), BF16),
             pltpu.VMEM((BUCKET, FF), BF16),
@@ -373,15 +394,13 @@
             pltpu.VMEM((D, FF), BF16),
             dma((3,)),
             dma,
-            dma((MICRO,)),
+            dma((UNITS,)),
             dma((2 * MICRO,)),
-            dma((slots + 1,)),
-            dma((slots + 1,)),
+            dma((slots,)),
+            dma((slots,)),
             dma((slots, GROUPS)),
-            dma,
-            dma((slots + 1,)),
-            dma,
-            dma,
+            dma((slots,)),
+            *[dma] * 6,
         ],
         compiler_params=pltpu.CompilerParams(has_side_effects=True, vmem_limit_bytes=56 << 20),
     )(inputs, cotangent, gate_weight, up_weight, down_weight, momentum, routes, routes, pairing)

time: 308 us -> 281 us (0.912)
  Pallas kernels: 308 us -> 280 us
    pallas_call x1, Pallas kernels: 305 us -> 278 us  [local(): pl.pallas_call(kernel, out_shape=(jax.ShapeDtypeStruct((1, 1, MICRO, ROWS...]
where the time goes in v3:
time: 281 us; the launch traced here: 280 us
  Pallas kernels  280 us (100%)
    pallas_call x1, Pallas kernels, local(): pl.pallas_call(kernel, out_shape=(jax.ShapeDtypeStruct((1, 1, MICRO, ROWS...  278 us

profile of v3, /device:TPU:25, one launch (start us, length us, event | category | flops | bytes accessed | tf_op | source)
XLA Modules:
  0.0 280.4 jit_solution(11490371847516108457)
XLA Ops:
  0.6 277.6 %shard_map.103 = (bf16[1,1,2,64,2048]{4,3,2,1,0:T(8,128)(2,1)}, bf16[1,1,2,64,2048]{4,3,2,1,0:T(8,128)(2,1)}, f32[1,1,128,768]{3,2,1,0:T(8,128)}) custom-call(bf16[1,2,8,2048]{3,2,1,0:T(8,128)(2,1)} %inp.1, bf16[1,2,8,2048]{3,2,1,0:T(8,128)(2,1)} %cot.1, bf16[1,1,2048,768]{3,2,1,0:T(8,128)(2,1)} %gate_h.1, bf16[1,1,2048,768]{3,2,1,0:T(8,128)(2,1)} %up_h.1, ...), custom_call_target="tpu_custom_call" | custom-call | tf_op jit(solution)/shard_map/pallas_call | solution.py:361
  278.2 2.2 shard_map.104

commit v4 on v3

--- a/solution.py
+++ b/solution.py
@@ -47,6 +47,30 @@
     loads = [pltpu.make_async_copy(h, v, w_sem.at[i])
              for i, (h, v) in enumerate(((gate_h.at[0, 0], gate), (up_h.at[0, 0], up), (down_h.at[0, 0], down)))]
 
+    barrier = pltpu.get_barrier_semaphore()
+
+    def signal(s, q):
+        pl.semaphore_signal(barrier, inc=1, device_id=dev(s, q), device_id_type=MESH)
+
+    def greet():
+        def body(q, carry):
+            for ahead in (3, 4, 5):
+                signal(lax.rem(t + ahead, SECTIONS), q)
+            return carry
+
+        for end in (0, SECTIONS - 1):
+            @pl.when(t != end)
+            def _():
+                signal(end, r)
+
+            @pl.when(t == end)
+            def _():
+                for s in range(SECTIONS):
+                    if s != end:
+                        signal(s, r)
+
+        lax.fori_loop(0, REPLICAS, body, 0, unroll=4)
+
     per = SECTIONS * MICRO // UNITS
 
     def gather(src, goal, sems):
@@ -64,12 +88,10 @@
                     src.at[0, m], place, gs_sem.at[sems + m], g_sem.at[unit],
                     device_id=dev(goal, r), device_id_type=MESH).start()
 
-    gather(inp, 0, 0)
     for load in loads:
         load.start()
-    gather(cot, SECTIONS - 1, MICRO)
     pltpu.make_async_copy(mom_h.at[0, 0], mom, m_sem).start()
-
+    greet()
     rv = routes_v[jnp.minimum(fwd_source, SECTIONS - 2)]
     goal_id = lax.broadcasted_iota(jnp.int32, (REPLICAS, REPLICAS), 0)
     from_id = lax.broadcasted_iota(jnp.int32, (REPLICAS, REPLICAS), 1)
@@ -80,6 +102,10 @@
     copy = pltpu.make_async_copy(inv_v, inv_s, i_sem)
     copy.start()
     copy.wait()
+    pl.semaphore_wait(barrier, jnp.where(jnp.logical_or(t == 0, t == SECTIONS - 1), 3 * REPLICAS + SECTIONS, 3 * REPLICAS + 2))
+    gather(inp, 0, 0)
+    gather(cot, SECTIONS - 1, MICRO)
+
 
     def assemble(m, slot):
         wait(gx.at[m], g_sem.at[m])
@@ -136,14 +162,15 @@
         def _():
             loads[2].wait()
 
-        for c in range(0, D, CHUNK):
-            res = xd[m, :, pl.ds(c, CHUNK)].astype(F32) + jnp.dot(
-                hidden, down[:, pl.ds(c, CHUNK)], preferred_element_type=F32)
-            out[m, :, pl.ds(c, CHUNK)] = res.astype(BF16)
+        for c in range(0, D, 4 * CHUNK):
+            res = xd[m, :, pl.ds(c, 4 * CHUNK)].astype(F32) + jnp.dot(
+                hidden, down[:, pl.ds(c, 4 * CHUNK)], preferred_element_type=F32)
+            out[m, :, pl.ds(c, 4 * CHUNK)] = res.astype(BF16)
 
             @pl.when(t < SECTIONS - 1)
             def _():
-                send_chunk(m, c // CHUNK, 1)
+                for o in range(4):
+                    send_chunk(m, c // CHUNK + o, 1)
 
         pltpu.make_async_copy(out.at[m], act_h.at[0, 0, m // 2, rows_of(m), :], o_sem).start()
         rinv_b[m] = jnp.broadcast_to(rinv, (UROWS, 128))
@@ -153,6 +180,19 @@
         a_b[m] = u * sg * (1.0 + g * (1.0 - sg))
         b_b[m] = gs
 
+    def accumulate(m, dg):
+        total[...] = total[...] + lax.dot_general(
+            nbuf[m], dg, (((0,), (0,)), ((), ())), preferred_element_type=F32)
+
+    def send_bucket():
+        wait(mom, m_sem)
+        fresh[...] = (BETA * mom[...] + (1.0 - BETA) * total[...]).astype(BF16)
+        for q in range(BP):
+            pltpu.make_async_remote_copy(
+                fresh.at[pl.ds(q // (FF // BC) * BR, BR), pl.ds(q % (FF // BC) * BC, BC)],
+                pb.at[r], pb_send, pb_recv,
+                device_id=dev(across, q), device_id_type=MESH).start()
+
     def backward(m):
         slot = UNITS + m
 
@@ -171,32 +211,44 @@
             dh = dh + jnp.dot(xd[slot, :, cols], down_t[cols, :], preferred_element_type=F32)
         dg = (dh * a_b[m]).astype(BF16)
         du = (dh * b_b[m]).astype(BF16)
+
+        @pl.when(t == 0)
+        def _():
+            accumulate(m, dg)
+
+        @pl.when(jnp.logical_and(t == 0, m == UNITS - 1))
+        def _():
+            send_bucket()
+
         both = dg.astype(F32) * g_b[m] + du.astype(F32) * u_b[m]
         corr = jnp.sum(both, axis=-1, keepdims=True) * (1.0 / D)
         rinv = rinv_b[m][:, :1]
-        for c in range(0, D, CHUNK):
-            cols = pl.ds(c, CHUNK)
+        for c in range(0, D, 4 * CHUNK):
+            cols = pl.ds(c, 4 * CHUNK)
             dn = jnp.dot(dg, gate_t[:, cols], preferred_element_type=F32) + jnp.dot(
                 du, up_t[:, cols], preferred_element_type=F32)
-            n = xd[m, :, pl.ds(c, CHUNK)].astype(F32) * rinv
-            res = xd[slot, :, pl.ds(c, CHUNK)].astype(F32) + rinv * (dn - n * corr)
-            out[slot, :, pl.ds(c, CHUNK)] = res.astype(BF16)
+            n = xd[m, :, pl.ds(c, 4 * CHUNK)].astype(F32) * rinv
+            res = xd[slot, :, pl.ds(c, 4 * CHUNK)].astype(F32) + rinv * (dn - n * corr)
+            out[slot, :, pl.ds(c, 4 * CHUNK)] = res.astype(BF16)
 
             @pl.when(t > 0)
             def _():
-                send_chunk(slot, c // CHUNK, -1)
+                for o in range(4):
+                    send_chunk(slot, c // CHUNK + o, -1)
 
         pltpu.make_async_copy(out.at[slot], ig_h.at[0, 0, m // 2, rows_of(m), :], o_sem).start()
-        part = lax.dot_general(nbuf[m], dg, (((0,), (0,)), ((), ())), preferred_element_type=F32)
-
-        total[...] = total[...] + part
+
+        @pl.when(t != 0)
+        def _():
+            accumulate(m, dg)
 
     def relay(slot, goal, index):
         wait(p1.at[slot], p1_recv.at[slot])
         sel[...] = p1[slot]
         place = xd.at[slot, pl.ds(pl.multiple_of(half * PR, PR), PR), pl.ds(pl.multiple_of(col * PC, PC), PC)]
 
-        def body(d, carry):
+        def body(i, carry):
+            d = lax.rem(i + r, REPLICAS)
             snd[slot, d] = sel[index(d)]
             pltpu.make_async_remote_copy(
                 snd.at[slot, d], place, p2_send.at[slot], p2_recv.at[slot, group],
@@ -282,13 +334,9 @@
 
     lax.fori_loop(0, 2 * UNITS, step, 0)
 
-    wait(mom, m_sem)
-    fresh[...] = (BETA * mom[...] + (1.0 - BETA) * total[...]).astype(BF16)
-    for q in range(BP):
-        pltpu.make_async_remote_copy(
-            fresh.at[pl.ds(q // (FF // BC) * BR, BR), pl.ds(q % (FF // BC) * BC, BC)],
-            pb.at[r], pb_send, pb_recv,
-            device_id=dev(across, q), device_id_type=MESH).start()
+    @pl.when(t != 0)
+    def _():
+        send_bucket()
 
     @pl.when(jnp.logical_not(early))
     def _():
@@ -402,7 +450,7 @@
             dma((slots,)),
             *[dma] * 6,
         ],
-        compiler_params=pltpu.CompilerParams(has_side_effects=True, vmem_limit_bytes=56 << 20),
+        compiler_params=pltpu.CompilerParams(collective_id=0, has_side_effects=True, vmem_limit_bytes=56 << 20),
     )(inputs, cotangent, gate_weight, up_weight, down_weight, momentum, routes, routes, pairing)
     return pl.pallas_call(
         hand_over,

time: 281 us -> 259 us (0.922)
  Pallas kernels: 280 us -> 258 us
    pallas_call x1, Pallas kernels: 278 us -> 256 us  [local(): pl.pallas_call(kernel, out_shape=(jax.ShapeDtypeStruct((1, 1, MICRO, ROWS...]
where the time goes in v4:
time: 259 us; the launch traced here: 258 us
  Pallas kernels  258 us (100%)
    pallas_call x1, Pallas kernels, local(): pl.pallas_call(kernel, out_shape=(jax.ShapeDtypeStruct((1, 1, MICRO, ROWS...  256 us

profile of v4, /device:TPU:25, one launch (start us, length us, event | category | flops | bytes accessed | tf_op | source)
XLA Modules:
  0.0 258.5 jit_solution(17201237640994566049)
XLA Ops:
  0.6 255.6 %shard_map.103 = (bf16[1,1,2,64,2048]{4,3,2,1,0:T(8,128)(2,1)}, bf16[1,1,2,64,2048]{4,3,2,1,0:T(8,128)(2,1)}, f32[1,1,128,768]{3,2,1,0:T(8,128)}) custom-call(bf16[1,2,8,2048]{3,2,1,0:T(8,128)(2,1)} %inp.1, bf16[1,2,8,2048]{3,2,1,0:T(8,128)(2,1)} %cot.1, bf16[1,1,2048,768]{3,2,1,0:T(8,128)(2,1)} %gate_h.1, bf16[1,1,2048,768]{3,2,1,0:T(8,128)(2,1)} %up_h.1, ...), custom_call_target="tpu_custom_call" | custom-call | tf_op jit(solution)/shard_map/pallas_call | solution.py:409
  256.3 2.2 shard_map.104

commit v5 on v4

--- a/solution.py
+++ b/solution.py
@@ -169,7 +169,7 @@
 
             @pl.when(t < SECTIONS - 1)
             def _():
-                for o in range(4):
+                for o in (0, 2, 1, 3):
                     send_chunk(m, c // CHUNK + o, 1)
 
         pltpu.make_async_copy(out.at[m], act_h.at[0, 0, m // 2, rows_of(m), :], o_sem).start()
@@ -233,7 +233,7 @@
 
             @pl.when(t > 0)
             def _():
-                for o in range(4):
+                for o in (0, 2, 1, 3):
                     send_chunk(slot, c // CHUNK + o, -1)
 
         pltpu.make_async_copy(out.at[slot], ig_h.at[0, 0, m // 2, rows_of(m), :], o_sem).start()

time: 259 us -> 256 us (0.988)
  no operation moved by 1% of the time
where the time goes in v5:
time: 256 us; the launch traced here: 257 us
  Pallas kernels  256 us (100%)
    pallas_call x1, Pallas kernels, local(): pl.pallas_call(kernel, out_shape=(jax.ShapeDtypeStruct((1, 1, MICRO, ROWS...  254 us

profile of v5, /device:TPU:25, one launch (start us, length us, event | category | flops | bytes accessed | tf_op | source)
XLA Modules:
  0.0 256.5 jit_solution(16366666598469301442)
XLA Ops:
  0.6 253.7 %shard_map.103 = (bf16[1,1,2,64,2048]{4,3,2,1,0:T(8,128)(2,1)}, bf16[1,1,2,64,2048]{4,3,2,1,0:T(8,128)(2,1)}, f32[1,1,128,768]{3,2,1,0:T(8,128)}) custom-call(bf16[1,2,8,2048]{3,2,1,0:T(8,128)(2,1)} %inp.1, bf16[1,2,8,2048]{3,2,1,0:T(8,128)(2,1)} %cot.1, bf16[1,1,2048,768]{3,2,1,0:T(8,128)(2,1)} %gate_h.1, bf16[1,1,2048,768]{3,2,1,0:T(8,128)(2,1)} %up_h.1, ...), custom_call_target="tpu_custom_call" | custom-call | tf_op jit(solution)/shard_map/pallas_call | solution.py:409
  254.4 2.2 shard_map.104
